TPU v7x, 32 devices: a whole 2x2x4 slice. The times are simulated.
32 devices in a mesh: row: 8 (over y, x, core), col: 4 (over z).
Axes of the slice: x: 2, y: 2, z: 4, core: 2. Of those that a mesh axis runs over, the one named last changes fastest.
Arguments:
- x_mat: float32 [512, 512], replicated, may hold values from -8 to 40, as said below
- y_inv: float32 [512, 512], replicated, may hold values from -8 to 40, as said below
- panel_blocks: bfloat16 [512, 4096], replicated, may hold values from -6 to 6
- panel_pos: int32 [512], replicated, may hold values from 0 to 63
- group_blocks: int32 [32, 2], replicated, may hold values from 0 to 63
- cons_blocks: bfloat16 [57344, 4096], P(('row', 'col')), may hold values from -6 to 6
- slot_block: int32 [57344], P(('row', 'col')), may hold values from 0 to 1
- slot_row: int32 [57344], P(('row', 'col')), may hold values from 0 to 32767, as said below
- group_size: int32 [32], P(('row', 'col')), may hold values from 768 to 1792, as said below
- trailing: float32 [32768, 2048], P('row', 'col'), may hold values from -6 to 6
Outputs:
- lower_panel: float32 [32768, 512], P(('row', 'col'))
- updated: float32 [32768, 2048], P('row', 'col')
Inputs may be any that keep to these rules, and one draw needn't show every extreme that they name: `x_mat`: symmetric positive definite. `y_inv`: symmetric positive definite. `slot_row`: over all groups, the live slots hold every row 0 to 32767 exactly once; the live slots of one group hold at most 56 rows of one aligned range of 1024 rows, and that most is reached in every draw; other slots hold arbitrary rows. `group_size`: the live slots of a group are its first slots; some group has exactly 1792 in every draw.
All inputs are finite; a program needn't handle non-finite values.
Results may differ from a plain program's by a relative error of at most 0.004.
Values may be sent and summed in bfloat16 or wider, within the bound.
A program may use at most 192 MiB of HBM per device.

v0:
```python
import math
import jax
import jax.numpy as jnp
from jax import lax
from jax.sharding import PartitionSpec as P


def build_h(values, position, x_mat, y_inv):
    highest = lax.Precision.HIGHEST
    matrix_order = x_mat.shape[0]
    block_size = math.isqrt(values.shape[0])
    block_count = matrix_order // block_size
    e_mat = values.reshape(block_size, block_size).astype(jnp.float32)
    row_start = position // block_count * block_size
    col_start = position % block_count * block_size
    x_left = lax.dynamic_slice_in_dim(x_mat, row_start, block_size, 1)
    x_right = lax.dynamic_slice_in_dim(x_mat, col_start, block_size, 1)
    y_low = lax.dynamic_slice_in_dim(y_inv, col_start, block_size, 0)
    y_high = lax.dynamic_slice_in_dim(y_inv, row_start, block_size, 0)
    term_one = jnp.dot(jnp.dot(x_left, e_mat, precision=highest), y_low, precision=highest)
    term_two = jnp.dot(jnp.dot(x_right, e_mat.T, precision=highest), y_high, precision=highest)
    g_mat = term_one + term_two
    h_mat = (g_mat + g_mat.T).astype(jnp.bfloat16)
    h_mat = h_mat.reshape(block_count, block_size, block_count, block_size).transpose(0, 2, 1, 3)
    return h_mat.reshape(block_count * block_count, block_size * block_size)


def body(
    x_mat,
    y_inv,
    panel_blocks,
    panel_pos,
    group_blocks,
    cons_blocks,
    slot_block,
    slot_row,
    group_size,
    trailing,
):
    rows_size = lax.axis_size("row")
    cols_size = lax.axis_size("col")
    devices = rows_size * cols_size
    col_index = lax.axis_index("col")
    device_id = lax.axis_index("row") * cols_size + col_index
    panel_cols = panel_blocks.shape[0]
    per_device = panel_cols // devices
    own_values = lax.dynamic_slice_in_dim(panel_blocks, device_id * per_device, per_device, 0)
    own_pos = lax.dynamic_slice_in_dim(panel_pos, device_id * per_device, per_device, 0)
    own_blocks = jax.vmap(build_h, in_axes=(0, 0, None, None))(own_values, own_pos, x_mat, y_inv)
    chosen = jnp.take(own_blocks, panel_pos, axis=1)
    column_part = jnp.einsum("if,nif->in", panel_blocks, chosen, preferred_element_type=jnp.float32)
    panel_schur = lax.all_gather(column_part, ("row", "col"), axis=1, tiled=True)
    symmetric = 0.5 * (panel_schur + panel_schur.T)
    diag_shift = 0.01 * jnp.mean(jnp.diagonal(symmetric))
    factor = jnp.linalg.cholesky(symmetric + diag_shift * jnp.eye(panel_cols, dtype=jnp.float32))
    slot_count = cons_blocks.shape[0]
    outgoing = jnp.take(own_blocks, group_blocks.T, axis=1)
    received = lax.all_to_all(outgoing, ("row", "col"), split_axis=2, concat_axis=2, tiled=True)
    running = jnp.zeros((slot_count, received.shape[2], received.shape[0]), jnp.float32)
    for slot_index in range(received.shape[1]):
        product_part = jnp.einsum(
            "sf,ndf->sdn", cons_blocks, received[:, slot_index], preferred_element_type=jnp.float32
        )
        running = jnp.where((slot_block == slot_index)[:, None, None], product_part, running)
    schur_rows = running.reshape(slot_count, panel_cols)
    sub_rows = trailing.shape[0] // cols_size
    base_share = sub_rows // devices
    spread = sub_rows - devices // 4 * base_share
    capacity = base_share + (spread + devices - 1) // devices
    live_slots = jnp.arange(slot_count, dtype=jnp.int32) < group_size[0]
    target = slot_row // sub_rows
    dest_hits = (
        (target[:, None] == jnp.arange(devices, dtype=jnp.int32)[None, :]) & live_slots[:, None]
    ).astype(jnp.int32)
    before = jnp.cumsum(dest_hits, axis=0) - dest_hits
    dest_rank = jnp.sum(before * dest_hits, axis=1)
    slot_place = jnp.where(live_slots, target * capacity + dest_rank, devices * capacity)
    send_rows = (
        jnp.zeros((devices * capacity, panel_cols), jnp.float32)
        .at[slot_place]
        .set(schur_rows, mode="drop")
    )
    send_local = (
        jnp.full((devices * capacity,), sub_rows, jnp.int32)
        .at[slot_place]
        .set(slot_row % sub_rows, mode="drop")
    )
    recv_rows, recv_local = (
        lax.all_to_all(
            send_rows.reshape(devices, capacity, panel_cols),
            ("row", "col"),
            split_axis=0,
            concat_axis=0,
            tiled=True,
        ),
        lax.all_to_all(
            send_local.reshape(devices, capacity),
            ("row", "col"),
            split_axis=0,
            concat_axis=0,
            tiled=True,
        ),
    )
    row_slab = (
        jnp.zeros((sub_rows, panel_cols), jnp.float32)
        .at[recv_local.reshape(-1)]
        .set(recv_rows.reshape(-1, panel_cols), mode="drop")
    )
    lower_slab = lax.linalg.triangular_solve(
        factor, row_slab, left_side=False, lower=True, transpose_a=True
    )
    all_rows = lax.all_gather(lower_slab, "col", axis=0, tiled=True)
    block_rows = trailing.shape[1] // rows_size
    own_rows = lax.dynamic_slice_in_dim(all_rows, col_index * block_rows, block_rows, 0)
    picked = lax.all_gather(own_rows, "row", axis=0, tiled=True)
    updated = trailing - jnp.dot(all_rows, picked.T, precision=lax.Precision.HIGHEST)
    return (lower_slab, updated)


def solution(mesh):
    return jax.shard_map(
        body,
        mesh=mesh,
        in_specs=(
            P(),
            P(),
            P(),
            P(),
            P(),
            P(("row", "col"), None),
            P(("row", "col")),
            P(("row", "col")),
            P(("row", "col")),
            P("row", "col"),
        ),
        out_specs=(P(("row", "col"), None), P("row", "col")),
        check_vma=False,
    )
```

profile of v0, /device:TPU:0, one launch (start us, length us, event | category | flops | bytes accessed | tf_op | source)
XLA Modules:
  0.0 992.5 jit_solution(9979744026841548414)
XLA Ops:
  10.2 2.5 broadcast.301.clone
  12.6 31.8 %while.5 = (s32[]{:T(128)}, f32[512,512]{1,0:T(8,128)S(1)}, s32[16,2]{0,1:T(2,128)S(1)}, f32[16,512,64]{2,1,0:T(8,128)}, s32[]{:T(128)}) while((s32[]{:T(128)}, f32[512,512]{1,0:T(8,128)S(1)}, s32[16,2]{0,1:T(2,128)S(1)}, f32[16,512,64]{2,1,0:T(8,128)}, s32[]{:T(128)}) %tuple.108), condition=%wide.while_cond, body=%wide.while_body.sunk | while | flops 2 | bytes 394329 | solution.py:16
  45.8 34.9 %while.6 = (s32[]{:T(128)}, f32[512,512]{1,0:T(8,128)}, s32[16,2]{0,1:T(2,128)S(1)}, f32[16,64,512]{2,1,0:T(8,128)S(1)}, s32[]{:T(128)}) while((s32[]{:T(128)}, f32[512,512]{1,0:T(8,128)}, s32[16,2]{0,1:T(2,128)S(1)}, f32[16,64,512]{2,1,0:T(8,128)S(1)}, s32[]{:T(128)}) %tuple.90), condition=%wide.while_cond.1, body=%wide.while_body.1.sunk | while | flops 2 | bytes 262241 | solution.py:18
  80.8 2.6 broadcast.301.clone.1
  83.4 35.3 %while.7 = (s32[]{:T(128)}, f32[512,512]{1,0:T(8,128)S(1)}, s32[16,2]{0,1:T(2,128)S(1)}, f32[16,512,64]{2,1,0:T(8,128)}, s32[]{:T(128)}) while((s32[]{:T(128)}, f32[512,512]{1,0:T(8,128)S(1)}, s32[16,2]{0,1:T(2,128)S(1)}, f32[16,512,64]{2,1,0:T(8,128)}, s32[]{:T(128)}) %tuple.109), condition=%wide.while_cond.2, body=%wide.while_body.2.sunk | while | flops 2 | bytes 394329 | solution.py:17
  118.7 5.0 fusion.71
  123.8 4.1 fusion.73
  129.4 47.0 %while.8 = (s32[]{:T(128)}, f32[512,512]{1,0:T(8,128)}, s32[16,2]{0,1:T(2,128)S(1)}, f32[16,64,512]{2,1,0:T(8,128)}, s32[]{:T(128)}) while((s32[]{:T(128)}, f32[512,512]{1,0:T(8,128)}, s32[16,2]{0,1:T(2,128)S(1)}, f32[16,64,512]{2,1,0:T(8,128)}, s32[]{:T(128)}) %tuple.110), condition=%wide.while_cond.3, body=%wide.while_body.3.sunk | while | flops 2 | bytes 263257 | solution.py:19
  176.4 17.1 %fusion.72 = f32[16,512,512]{2,1,0:T(8,128)} fusion(f32[16,512,64]{1,2,0:T(8,128)S(1)} %fusion.71, f32[16,64,512]{2,1,0:T(8,128)} %copy-done.3), kind=kOutput, calls=%fused_computation.160 | convolution fusion | flops 3221225472 | bytes 20971520 | tf_op jit(solution)/shard_map/vmap()/dot_general | solution.py:20
  193.5 18.9 %convolution_add_fusion = f32[16,512,512]{2,1,0:T(8,128)} fusion(f32[16,512,512]{2,1,0:T(8,128)} %fusion.72, f32[16,512,64]{1,2,0:T(8,128)S(1)} %copy-done.2, f32[16,64,512]{2,1,0:T(8,128)S(1)} %copy-done.4), kind=kOutput, calls=%fused_computation.28 | convolution fusion | flops 3225419776 | bytes 37748736 | tf_op jit(solution)/shard_map/vmap()/dot_general | solution.py:21
  212.4 17.6 %copy.62 = f32[16,512,512]{1,2,0:T(8,128)} copy(f32[16,512,512]{2,1,0:T(8,128)} %convolution_add_fusion) | data formatting | bytes 33554432 | tf_op jit(solution)/shard_map/vmap()/add | solution.py:22
  230.0 15.1 %fusion.5 = bf16[16,512,512]{2,1,0:T(8,128)(2,1)} fusion(f32[16,512,512]{2,1,0:T(8,128)} %convolution_add_fusion, f32[16,512,512]{1,2,0:T(8,128)} %copy.62), kind=kLoop, calls=%fused_computation.22 | loop fusion | flops 8388608 | bytes 41943040 | tf_op jit(solution)/shard_map/vmap()/convert_element_type | solution.py:23
  245.0 21.2 %reshape.134 = bf16[16,8,64,8,64]{4,3,2,1,0:T(8,128)(2,1)} reshape(bf16[16,512,512]{2,1,0:T(8,128)(2,1)} %fusion.5) | data formatting | bytes 16777216 | tf_op jit(solution)/shard_map/vmap()/reshape | solution.py:24
  266.3 15.1 %copy.93 = bf16[16,8,64,8,64]{4,2,3,1,0:T(8,128)(2,1)} copy(bf16[16,8,64,8,64]{4,3,2,1,0:T(8,128)(2,1)} %reshape.134) | data formatting | bytes 16777216 | tf_op jit(solution)/shard_map/vmap()/reshape | solution.py:24
  281.3 22.6 %reshape.135 = bf16[16,64,4096]{2,1,0:T(8,128)(2,1)} reshape(bf16[16,8,8,64,64]{4,3,2,1,0:T(8,128)(2,1)} %bitcast.160) | data formatting | bytes 16777216 | tf_op jit(solution)/shard_map/vmap()/reshape | solution.py:25
  303.9 11.2 %copy.64 = bf16[16,64,4096]{2,0,1:T(8,128)(2,1)} copy(bf16[16,64,4096]{2,1,0:T(8,128)(2,1)} %reshape.135) | data formatting | bytes 16777216 | tf_op jit(solution)/shard_map/vmap()/reshape | solution.py:25
  315.2 9.5 gather_fusion
  324.7 7.6 select_bitcast_fusion
  332.3 7.8 copy.65
  340.1 7.4 all-to-all-start.1
  347.7 28.5 %gather_fusion.1 = bf16[512,16,4096]{2,1,0:T(8,128)(2,1)} fusion(bf16[16,64,4096]{2,0,1:T(8,128)(2,1)} %copy.64, s32[1024]{0:T(1024)S(1)} %pad_clamp_fusion), kind=kCustom, calls=%fused_computation.1 | custom fusion | bytes 134219776 | tf_op jit(solution)/shard_map/jit(_take)/gather | solution.py:50
  376.2 30.4 %fusion = f32[512,1,16]{2,1,0:T(1,128)S(1)} fusion(bf16[512,16,4096]{2,1,0:T(8,128)(2,1)} %gather_fusion.1, pred[512]{0:T(512)(128)(4,1)S(1)} %compare_and_fusion, bf16[512,4096,1]{1,0,2:T(8,128)(2,1)} %bitcast.170), kind=kOutput, calls=%fused_computation.16 | convolution fusion | flops 100663296 | bytes 71336448 | tf_op jit(solution)/shard_map/if,nif->in/dot_general | solution.py:51
  408.1 9.1 reduce-window.6
  417.9 7.1 scatter_custom_fusion
  425.7 108.3 %all-to-all-done.1 = bf16[16,2,32,4096]{3,0,1,2:T(8,128)(2,1)} async-done(((bf16[16,2,32,4096]{3,0,1,2:T(8,128)(2,1)}), bf16[16,2,32,4096]{3,0,1,2:T(8,128)(2,1)}, u32[]{:S(2)}, u32[]{:S(2)}) %all-to-all-start.1) | async-done | bytes 8388640 | tf_op jit(solution)/shard_map/all_to_all | solution.py:58
  534.0 8.5 all-to-all-start
  542.5 5.2 fusion.68
  547.8 15.3 %fusion.6 = f32[16,32,1792]{2,1,0:T(8,128)} fusion(bf16[1792,4096]{1,0:T(8,128)(2,1)} %param.15, bf16[16,1,32,4096]{3,0,1,2:T(8,128)(2,1)S(1)} %get-tuple-element.97), kind=kOutput, calls=%fused_computation.24 | convolution fusion | flops 7516192768 | bytes 22544384 | tf_op jit(solution)/shard_map/sf,ndf->sdn/dot_general | solution.py:61
  563.0 18.1 %select_bitcast_fusion.1 = f32[1792,32,16]{0,1,2:T(8,128)} fusion(f32[16,32,1792]{2,1,0:T(8,128)} %fusion.6, bf16[1792,4096]{1,0:T(8,128)(2,1)} %param.15, bf16[16,1,32,4096]{3,0,1,2:T(8,128)(2,1)} %get-tuple-element.96, pred[1792]{0:T(1024)(128)(4,1)S(1)} %get-tuple-element.109, pred[1792]{0:T(1024)(128)(4,1)S(1)} %get-tuple-element.108), kind=kOutput, calls=%fused_computation.34 | convolution fusion | flops 7518027776 | bytes 26217984 | tf_op jit(solution)/shard_map/sf,ndf->sdn/dot_general | solution.py:61
  581.1 6.0 copy.68
  587.1 5.1 copy.69
  592.2 13.1 %scatter_custom_fusion.1 = f32[1792,512]{1,0:T(8,128)} fusion(s32[1792]{0:T(1024)S(1)} %compare_select_fusion.1, f32[1792,512]{1,0:T(8,128)} %copy.69, f32[]{:T(128)} %constant.245.clone.1), kind=kCustom, calls=%fused_computation.36 | custom fusion | bytes 3670528 | tf_op jit(solution)/shard_map/scatter | solution.py:81
  605.4 6.1 all-to-all-start.2
  615.8 4.9 gather_fusion.2
  622.6 11.7 %cholesky.103 = f32[128,128]{1,0:T(8,128)S(1)} custom-call(f32[128,128]{1,0:T(8,128)S(1)} %cholesky.263), custom_call_target="Cholesky" | custom-call | tf_op jit(solution)/shard_map/jit(cholesky)/cholesky | solution.py:55
  634.5 9.8 custom-call.30
  645.0 11.7 %cholesky.215 = f32[128,128]{1,0:T(8,128)S(1)} custom-call(f32[128,128]{1,0:T(8,128)S(1)} %cholesky.267), custom_call_target="Cholesky" | custom-call | tf_op jit(solution)/shard_map/jit(cholesky)/cholesky | solution.py:55
  656.7 10.0 %custom-call.31 = f32[1,128,128]{1,2,0:T(8,128)S(1)} custom-call(f32[1,128,128]{2,1,0:T(8,128)S(1)} %get-tuple-element.104), custom_call_target="InvertDiagBlocksLowerTriangular" | custom-call | tf_op jit(solution)/shard_map/jit(cholesky)/cholesky | solution.py:55
  667.4 11.7 %cholesky.236 = f32[128,128]{1,0:T(8,128)S(1)} custom-call(f32[128,128]{1,0:T(8,128)S(1)} %cholesky.272), custom_call_target="Cholesky" | custom-call | tf_op jit(solution)/shard_map/jit(cholesky)/cholesky | solution.py:55
  679.1 9.8 custom-call.32
  689.5 11.7 %cholesky.253 = f32[128,128]{1,0:T(8,128)S(1)} custom-call(f32[128,128]{1,0:T(8,128)S(1)} %convolution_subtract_fusion.5), custom_call_target="Cholesky" | custom-call | tf_op jit(solution)/shard_map/jit(cholesky)/cholesky | solution.py:55
  706.6 10.6 %while.9 = (s32[]{:T(128)}, f32[512,512]{1,0:T(8,128)S(1)}, s32[4,2]{0,1:T(2,128)S(1)}, f32[4,128,128]{2,1,0:T(8,128)}, s32[]{:T(128)}) while((s32[]{:T(128)}, f32[512,512]{1,0:T(8,128)S(1)}, s32[4,2]{0,1:T(2,128)S(1)}, f32[4,128,128]{2,1,0:T(8,128)}, s32[]{:T(128)}) %tuple.99), condition=%wide.while_cond.4, body=%wide.while_body.4.sunk | while | flops 2 | bytes 132705 | solution.py:109
  717.2 40.1 %custom-call.33 = f32[4,128,128]{1,2,0:T(8,128)S(1)} custom-call(f32[4,128,128]{2,1,0:T(8,128)} %get-tuple-element.41), custom_call_target="InvertDiagBlocksLowerTriangular" | custom-call | tf_op jit(solution)/shard_map/triangular_solve | solution.py:109
  757.4 11.6 %scatter_custom_fusion.2 = f32[1024,512]{1,0:T(8,128)S(1)} fusion(s32[1792]{0:T(1024)S(1)} %fusion.57, f32[1792,512]{1,0:T(8,128)} %bitcast.17, f32[]{:T(128)} %constant.245.clone.1), kind=kCustom, calls=%fused_computation.63 | custom fusion | bytes 2097664 | tf_op jit(solution)/shard_map/scatter | solution.py:107
  773.7 2.8 fusion.21
  779.0 150.6 %all-gather.6.cloned.1.call-done = f32[4096,512]{0,1:T(8,128)} async-done(((f32[1024,512]{0,1:T(8,128)}), f32[4096,512]{0,1:T(8,128)}) %all-gather.6.cloned.1.call-update) | async-done | bytes 8388624 | tf_op jit(solution)/shard_map/all_gather | solution.py:112
  933.4 20.4 %all-gather.8.cloned.1.call-done = f32[512,512]{1,0:T(8,128)} async-done(((f32[64,512]{1,0:T(8,128)}), f32[512,512]{1,0:T(8,128)}) %all-gather.8.cloned.1.call-update) | async-done | bytes 1048592 | tf_op jit(solution)/shard_map/all_gather | solution.py:115
  953.7 31.8 %convolution_subtract_fusion = f32[4096,512]{1,0:T(8,128)} fusion(f32[4096,512]{1,0:T(8,128)} %param.19, f32[4096,512]{0,1:T(8,128)} %all-gather.6.cloned.1.call-done, f32[512,512]{1,0:T(8,128)} %all-gather.8.cloned.1.call-done), kind=kOutput, calls=%fused_computation.31 | convolution fusion | flops 12886999040 | bytes 26214400 | tf_op jit(solution)/shard_map/dot_general | solution.py:116
  (302 shorter events, 188.9 us)
Async XLA Ops:
  7.2 5.5 copy-start.5
  80.8 38.0 %copy-start.3 = (f32[16,64,512]{2,1,0:T(8,128)}, f32[16,64,512]{2,1,0:T(8,128)S(1)}, u32[]{:S(2)}) copy-start(f32[16,64,512]{2,1,0:T(8,128)S(1)} %get-tuple-element.17) | copy-start | bytes 6291460
  118.7 5.0 copy-start.1
  176.4 17.1 %copy-start.2 = (f32[16,512,64]{1,2,0:T(8,128)S(1)}, f32[16,512,64]{1,2,0:T(8,128)}, u32[]{:S(2)}) copy-start(f32[16,512,64]{1,2,0:T(8,128)} %fusion.73) | copy-start | bytes 6291460
  176.4 17.1 %copy-start.4 = (f32[16,64,512]{2,1,0:T(8,128)S(1)}, f32[16,64,512]{2,1,0:T(8,128)}, u32[]{:S(2)}) copy-start(f32[16,64,512]{2,1,0:T(8,128)} %get-tuple-element.33) | copy-start | bytes 6291460
  340.1 7.5 copy-start.6
  340.1 193.9 %all-to-all-start.1 = ((bf16[16,2,32,4096]{3,0,1,2:T(8,128)(2,1)}), bf16[16,2,32,4096]{3,0,1,2:T(8,128)(2,1)}, u32[]{:S(2)}, u32[]{:S(2)}) async-start(bf16[16,2,32,4096]{3,0,1,2:T(8,128)(2,1)} %copy.65), calls=%async_computation.1 | async-start | bytes 16777216 | tf_op jit(solution)/shard_map/all_to_all | solution.py:58
  347.6 265.2 %all-gather.4.cloned.1.call-start = ((), (), s32[]{:S(2)}) async-start(), calls=%async_computation.3 | async-start | bytes 1081344 | tf_op jit(solution)/shard_map/all_gather | solution.py:52
  376.2 31.8 %copy-start.7 = (s32[1792]{0:T(1024)S(1)}, s32[1792]{0:T(1024)}, u32[]{:S(2)}) copy-start(s32[1792]{0:T(1024)} %param.17) | copy-start | bytes 21508
  376.2 49.5 %copy-start.8 = (s32[1792]{0:T(1024)S(1)}, s32[1792]{0:T(1024)}, u32[]{:S(2)}) copy-start(s32[1792]{0:T(1024)} %param.16) | copy-start | bytes 21508
  534.0 71.4 %all-to-all-start = ((s32[32,1,56]{2,1,0:T(1,128)}), s32[32,1,56]{2,1,0:T(1,128)S(1)}, u32[]{:S(2)}, u32[]{:S(2)}) async-start(s32[32,1,56]{2,1,0:T(1,128)} %all_to_all.12), calls=%async_computation | async-start | bytes 32768 | tf_op jit(solution)/shard_map/all_to_all | solution.py:96
  605.4 152.0 %all-to-all-start.2 = ((f32[32,56,512]{2,1,0:T(8,128)}), f32[32,56,512]{2,1,0:T(8,128)}, u32[]{:S(2)}, u32[]{:S(2)}) async-start(f32[32,56,512]{2,1,0:T(8,128)} %bitcast.164), calls=%async_computation.2 | async-start | bytes 7340032 | tf_op jit(solution)/shard_map/all_to_all | solution.py:89
  611.4 318.2 %all-gather.6.cloned.1.call-start = ((), (), s32[]{:S(2)}) async-start(), calls=%async_computation.4 | async-start | bytes 10485760 | tf_op jit(solution)/shard_map/all_gather | solution.py:112
  778.7 152.8 %copy-start = (f32[1024,512]{0,1:T(8,128)S(1)}, f32[1024,512]{0,1:T(8,128)}, u32[]{:S(2)}) copy-start(f32[1024,512]{0,1:T(8,128)} %pad_maximum_fusion) | copy-start | bytes 6291460
  778.7 175.0 %all-gather.8.cloned.1.call-start = ((), (), s32[]{:S(2)}) async-start(), calls=%async_computation.5 | async-start | bytes 1179648 | tf_op jit(solution)/shard_map/all_gather | solution.py:115
Sparse Core Ops, SparseCore 0:
  407.5 96.1 all-gather.3
  778.8 150.7 all-gather.5
  932.1 21.5 all-gather.7
where the time goes:
time: 1000 us; the launch traced here: 992 us
  local copies, waits for them, and re-layouts  362 us (36%)
  waiting for transfers between devices  279 us (28%)
  other arithmetic  159 us (16%)
  matrix products  151 us (15%)
  starting transfers between devices  22.4 us (2%)
  between operations  18.5 us (2%)
    all_gather x1, waiting for transfers between devices, body(): all_rows = lax.all_gather(lower_slab, 'col', axis=0, tiled=True)  151 us
    gather x192, local copies, waits for them, and re-layouts  149 us
    all_to_all x1, waiting for transfers between devices, body(): lax.all_to_all(outgoing, ('row', 'col'), split_axis=2, concat_axis=2, til...  108 us
    another operation x15, other arithmetic, body(): jnp.linalg.cholesky(symmetric + diag_shift * jnp.eye(panel_cols, dtype=jn...  79.2 us
    another operation x4, other arithmetic, body(): lax.linalg.triangular_solve(factor, row_slab, left_side=False, lower=True...  41.8 us
    reshape x2, local copies, waits for them, and re-layouts, build_h(): h_mat.reshape(block_count, block_size, block_count, block_size)  36.3 us
    reshape x2, local copies, waits for them, and re-layouts, build_h(): return h_mat.reshape(block_count * block_count, block_size * block_size)  33.7 us
    dot_general x2, matrix products, body(): jnp.einsum('sf,ndf->sdn', cons_blocks, received[:, slot_index], preferred...  33.3 us
  transfers between devices with their start and end apart: 6, of which 3 were waited for; matrix products, arithmetic and copies ran while one was open for 29% of the time, Pallas kernels for 0%

commit v1 on v0

--- a/solution.py
+++ b/solution.py
@@ -3,6 +3,18 @@
 import jax.numpy as jnp
 from jax import lax
 from jax.sharding import PartitionSpec as P
+
+
+def gather_by_bits(x, axis, dim):
+    ways, here = (lax.axis_size(axis), lax.axis_index(axis))
+    grown, reach = (x, 1)
+    while reach < ways:
+        theirs = lax.ppermute(grown, axis, [(d, d ^ reach) for d in range(ways)])
+        mine_first = jnp.concatenate([grown, theirs], axis=dim)
+        theirs_first = jnp.concatenate([theirs, grown], axis=dim)
+        grown = jnp.where(here & reach == 0, mine_first, theirs_first)
+        reach = 2 * reach
+    return grown
 
 
 def build_h(values, position, x_mat, y_inv):
@@ -109,7 +121,7 @@
     lower_slab = lax.linalg.triangular_solve(
         factor, row_slab, left_side=False, lower=True, transpose_a=True
     )
-    all_rows = lax.all_gather(lower_slab, "col", axis=0, tiled=True)
+    all_rows = gather_by_bits(lower_slab, "col", 0)
     block_rows = trailing.shape[1] // rows_size
     own_rows = lax.dynamic_slice_in_dim(all_rows, col_index * block_rows, block_rows, 0)
     picked = lax.all_gather(own_rows, "row", axis=0, tiled=True)

time: 1000 us -> 1100 us (1.10)
  waiting for transfers between devices: 279 us -> 358 us
  other arithmetic: 159 us -> 172 us
    ppermute x0 -> x2, waiting for transfers between devices: none -> 226 us  [gather_by_bits(): theirs = lax.ppermute(grown, axis, [(d, d ^ reach) for d in range(ways)])]
    all_gather x1 -> x0, waiting for transfers between devices: 151 us -> none  [body(): all_rows = lax.all_gather(lower_slab, 'col', axis=0, tiled=True)]
    select_n x0 -> x2, other arithmetic: none -> 14.3 us  [gather_by_bits(): grown = jnp.where(here & reach == 0, mine_first, theirs_first)]
  transfers between devices with their start and end apart: 6 -> 7, of which waited for: 3 -> 4; matrix products, arithmetic and copies ran while one was open for 29% -> 26% of each run, Pallas kernels for 0% -> 0%
where the time goes in v1:
time: 1100 us; the launch traced here: 1090 us
  local copies, waits for them, and re-layouts  364 us (33%)
  waiting for transfers between devices  358 us (33%)
  other arithmetic  172 us (16%)
  matrix products  154 us (14%)
  starting transfers between devices  26.6 us (2%)
  between operations  18.8 us (2%)
    ppermute x2, waiting for transfers between devices, gather_by_bits(): theirs = lax.ppermute(grown, axis, [(d, d ^ reach) for d in range(ways)])  226 us
    gather x192, local copies, waits for them, and re-layouts  149 us
    all_to_all x1, waiting for transfers between devices, body(): lax.all_to_all(outgoing, ('row', 'col'), split_axis=2, concat_axis=2, til...  108 us
    another operation x15, other arithmetic, body(): jnp.linalg.cholesky(symmetric + diag_shift * jnp.eye(panel_cols, dtype=jn...  79.3 us
    another operation x4, other arithmetic, body(): lax.linalg.triangular_solve(factor, row_slab, left_side=False, lower=True...  40.5 us
    reshape x2, local copies, waits for them, and re-layouts, build_h(): h_mat.reshape(block_count, block_size, block_count, block_size)  36.3 us
    reshape x2, local copies, waits for them, and re-layouts, build_h(): return h_mat.reshape(block_count * block_count, block_size * block_size)  33.7 us
    dot_general x2, matrix products, body(): jnp.einsum('sf,ndf->sdn', cons_blocks, received[:, slot_index], preferred...  33.3 us
  transfers between devices with their start and end apart: 7, of which 4 were waited for; matrix products, arithmetic and copies ran while one was open for 26% of the time, Pallas kernels for 0%

profile of v1, /device:TPU:0, one launch (start us, length us, event | category | flops | bytes accessed | tf_op | source)
XLA Modules:
  0.0 1093.4 jit_solution(9905842228860316831)
XLA Ops:
  12.6 31.8 %while.5 = (s32[]{:T(128)}, f32[512,512]{1,0:T(8,128)S(1)}, s32[16,2]{0,1:T(2,128)S(1)}, f32[16,512,64]{2,1,0:T(8,128)}, s32[]{:T(128)}) while((s32[]{:T(128)}, f32[512,512]{1,0:T(8,128)S(1)}, s32[16,2]{0,1:T(2,128)S(1)}, f32[16,512,64]{2,1,0:T(8,128)}, s32[]{:T(128)}) %tuple.106), condition=%wide.while_cond, body=%wide.while_body.sunk | while | flops 2 | bytes 394329 | solution.py:28
  45.8 34.9 %while.6 = (s32[]{:T(128)}, f32[512,512]{1,0:T(8,128)}, s32[16,2]{0,1:T(2,128)S(1)}, f32[16,64,512]{2,1,0:T(8,128)S(1)}, s32[]{:T(128)}) while((s32[]{:T(128)}, f32[512,512]{1,0:T(8,128)}, s32[16,2]{0,1:T(2,128)S(1)}, f32[16,64,512]{2,1,0:T(8,128)S(1)}, s32[]{:T(128)}) %tuple.90), condition=%wide.while_cond.1, body=%wide.while_body.1.sunk | while | flops 2 | bytes 262241 | solution.py:30
  83.4 35.3 %while.7 = (s32[]{:T(128)}, f32[512,512]{1,0:T(8,128)S(1)}, s32[16,2]{0,1:T(2,128)S(1)}, f32[16,512,64]{2,1,0:T(8,128)}, s32[]{:T(128)}) while((s32[]{:T(128)}, f32[512,512]{1,0:T(8,128)S(1)}, s32[16,2]{0,1:T(2,128)S(1)}, f32[16,512,64]{2,1,0:T(8,128)}, s32[]{:T(128)}) %tuple.107), condition=%wide.while_cond.2, body=%wide.while_body.2.sunk | while | flops 2 | bytes 394329 | solution.py:29
  118.7 5.0 fusion.71
  123.8 4.1 fusion.73
  129.4 47.0 %while.8 = (s32[]{:T(128)}, f32[512,512]{1,0:T(8,128)}, s32[16,2]{0,1:T(2,128)S(1)}, f32[16,64,512]{2,1,0:T(8,128)}, s32[]{:T(128)}) while((s32[]{:T(128)}, f32[512,512]{1,0:T(8,128)}, s32[16,2]{0,1:T(2,128)S(1)}, f32[16,64,512]{2,1,0:T(8,128)}, s32[]{:T(128)}) %tuple.108), condition=%wide.while_cond.3, body=%wide.while_body.3.sunk | while | flops 2 | bytes 263257 | solution.py:31
  176.4 17.1 %fusion.72 = f32[16,512,512]{2,1,0:T(8,128)} fusion(f32[16,512,64]{1,2,0:T(8,128)S(1)} %fusion.71, f32[16,64,512]{2,1,0:T(8,128)} %copy-done.3), kind=kOutput, calls=%fused_computation.162 | convolution fusion | flops 3221225472 | bytes 20971520 | tf_op jit(solution)/shard_map/vmap()/dot_general | solution.py:32
  193.5 19.1 %convolution_add_fusion = f32[16,512,512]{2,1,0:T(8,128)} fusion(f32[16,512,512]{2,1,0:T(8,128)} %fusion.72, f32[16,512,64]{1,2,0:T(8,128)S(1)} %copy-done.2, f32[16,64,512]{2,1,0:T(8,128)S(1)} %copy-done.4), kind=kOutput, calls=%fused_computation.28 | convolution fusion | flops 3225419776 | bytes 37748736 | tf_op jit(solution)/shard_map/vmap()/dot_general | solution.py:33
  212.6 17.6 %copy.62 = f32[16,512,512]{1,2,0:T(8,128)} copy(f32[16,512,512]{2,1,0:T(8,128)} %convolution_add_fusion) | data formatting | bytes 33554432 | tf_op jit(solution)/shard_map/vmap()/add | solution.py:34
  230.2 15.1 %fusion.5 = bf16[16,512,512]{2,1,0:T(8,128)(2,1)} fusion(f32[16,512,512]{2,1,0:T(8,128)} %convolution_add_fusion, f32[16,512,512]{1,2,0:T(8,128)} %copy.62), kind=kLoop, calls=%fused_computation.22 | loop fusion | flops 8388608 | bytes 41943040 | tf_op jit(solution)/shard_map/vmap()/convert_element_type | solution.py:35
  245.3 21.2 %reshape.134 = bf16[16,8,64,8,64]{4,3,2,1,0:T(8,128)(2,1)} reshape(bf16[16,512,512]{2,1,0:T(8,128)(2,1)} %fusion.5) | data formatting | bytes 16777216 | tf_op jit(solution)/shard_map/vmap()/reshape | solution.py:36
  266.5 15.1 %copy.93 = bf16[16,8,64,8,64]{4,2,3,1,0:T(8,128)(2,1)} copy(bf16[16,8,64,8,64]{4,3,2,1,0:T(8,128)(2,1)} %reshape.134) | data formatting | bytes 16777216 | tf_op jit(solution)/shard_map/vmap()/reshape | solution.py:36
  281.6 22.6 %reshape.135 = bf16[16,64,4096]{2,1,0:T(8,128)(2,1)} reshape(bf16[16,8,8,64,64]{4,3,2,1,0:T(8,128)(2,1)} %bitcast.160) | data formatting | bytes 16777216 | tf_op jit(solution)/shard_map/vmap()/reshape | solution.py:37
  304.1 11.2 %copy.64 = bf16[16,64,4096]{2,0,1:T(8,128)(2,1)} copy(bf16[16,64,4096]{2,1,0:T(8,128)(2,1)} %reshape.135) | data formatting | bytes 16777216 | tf_op jit(solution)/shard_map/vmap()/reshape | solution.py:37
  315.4 9.3 gather_fusion
  324.7 7.6 select_bitcast_fusion
  332.3 7.8 copy.65
  340.1 7.5 all-to-all-start.1
  347.6 28.5 %gather_fusion.1 = bf16[512,16,4096]{2,1,0:T(8,128)(2,1)} fusion(bf16[16,64,4096]{2,0,1:T(8,128)(2,1)} %copy.64, s32[1024]{0:T(1024)S(1)} %pad_clamp_fusion), kind=kCustom, calls=%fused_computation.1 | custom fusion | bytes 134219776 | tf_op jit(solution)/shard_map/jit(_take)/gather | solution.py:62
  376.2 30.4 %fusion = f32[512,1,16]{2,1,0:T(1,128)S(1)} fusion(bf16[512,16,4096]{2,1,0:T(8,128)(2,1)} %gather_fusion.1, pred[512]{0:T(512)(128)(4,1)S(1)} %compare_and_fusion, bf16[512,4096,1]{1,0,2:T(8,128)(2,1)} %bitcast.170), kind=kOutput, calls=%fused_computation.16 | convolution fusion | flops 100663296 | bytes 71336448 | tf_op jit(solution)/shard_map/if,nif->in/dot_general | solution.py:63
  408.1 9.1 reduce-window.6
  417.9 7.1 scatter_custom_fusion
  425.7 108.3 %all-to-all-done.1 = bf16[16,2,32,4096]{3,0,1,2:T(8,128)(2,1)} async-done(((bf16[16,2,32,4096]{3,0,1,2:T(8,128)(2,1)}), bf16[16,2,32,4096]{3,0,1,2:T(8,128)(2,1)}, u32[]{:S(2)}, u32[]{:S(2)}) %all-to-all-start.1) | async-done | bytes 8388640 | tf_op jit(solution)/shard_map/all_to_all | solution.py:70
  534.0 8.8 all-to-all-start
  542.8 5.2 fusion.68
  548.0 15.3 %fusion.6 = f32[16,32,1792]{2,1,0:T(8,128)} fusion(bf16[1792,4096]{1,0:T(8,128)(2,1)} %param.15, bf16[16,1,32,4096]{3,0,1,2:T(8,128)(2,1)S(1)} %get-tuple-element.97), kind=kOutput, calls=%fused_computation.24 | convolution fusion | flops 7516192768 | bytes 22544384 | tf_op jit(solution)/shard_map/sf,ndf->sdn/dot_general | solution.py:73
  563.2 18.1 %select_bitcast_fusion.1 = f32[1792,32,16]{0,1,2:T(8,128)} fusion(f32[16,32,1792]{2,1,0:T(8,128)} %fusion.6, bf16[1792,4096]{1,0:T(8,128)(2,1)} %param.15, bf16[16,1,32,4096]{3,0,1,2:T(8,128)(2,1)} %get-tuple-element.96, pred[1792]{0:T(1024)(128)(4,1)S(1)} %get-tuple-element.109, pred[1792]{0:T(1024)(128)(4,1)S(1)} %get-tuple-element.108), kind=kOutput, calls=%fused_computation.36 | convolution fusion | flops 7518027776 | bytes 26217984 | tf_op jit(solution)/shard_map/sf,ndf->sdn/dot_general | solution.py:73
  581.3 6.0 copy.68
  587.3 5.1 copy.69
  592.4 13.1 %scatter_custom_fusion.1 = f32[1792,512]{1,0:T(8,128)} fusion(s32[1792]{0:T(1024)S(1)} %compare_select_fusion.1, f32[1792,512]{1,0:T(8,128)} %copy.69, f32[]{:T(128)} %constant.247.clone.1), kind=kCustom, calls=%fused_computation.38 | custom fusion | bytes 3670528 | tf_op jit(solution)/shard_map/scatter | solution.py:93
  605.6 6.1 all-to-all-start.2
  616.1 4.7 gather_fusion.2
  622.8 11.7 %cholesky.103 = f32[128,128]{1,0:T(8,128)S(1)} custom-call(f32[128,128]{1,0:T(8,128)S(1)} %cholesky.263), custom_call_target="Cholesky" | custom-call | tf_op jit(solution)/shard_map/jit(cholesky)/cholesky | solution.py:67
  634.7 9.8 custom-call.30
  645.2 11.7 %cholesky.215 = f32[128,128]{1,0:T(8,128)S(1)} custom-call(f32[128,128]{1,0:T(8,128)S(1)} %cholesky.267), custom_call_target="Cholesky" | custom-call | tf_op jit(solution)/shard_map/jit(cholesky)/cholesky | solution.py:67
  656.9 10.2 custom-call.31
  667.8 11.7 %cholesky.236 = f32[128,128]{1,0:T(8,128)S(1)} custom-call(f32[128,128]{1,0:T(8,128)S(1)} %cholesky.272), custom_call_target="Cholesky" | custom-call | tf_op jit(solution)/shard_map/jit(cholesky)/cholesky | solution.py:67
  679.5 9.8 custom-call.32
  690.0 11.7 %cholesky.253 = f32[128,128]{1,0:T(8,128)S(1)} custom-call(f32[128,128]{1,0:T(8,128)S(1)} %convolution_subtract_fusion.5), custom_call_target="Cholesky" | custom-call | tf_op jit(solution)/shard_map/jit(cholesky)/cholesky | solution.py:67
  707.1 10.1 while.9
  717.1 40.2 %custom-call.33 = f32[4,128,128]{1,2,0:T(8,128)S(1)} custom-call(f32[4,128,128]{2,1,0:T(8,128)} %get-tuple-element.41), custom_call_target="InvertDiagBlocksLowerTriangular" | custom-call | tf_op jit(solution)/shard_map/triangular_solve | solution.py:121
  757.3 11.6 %scatter_custom_fusion.2 = f32[1024,512]{1,0:T(8,128)S(1)} fusion(s32[1792]{0:T(1024)S(1)} %fusion.57, f32[1792,512]{1,0:T(8,128)} %bitcast.17, f32[]{:T(128)} %constant.247.clone.1), kind=kCustom, calls=%fused_computation.65 | custom fusion | bytes 2097664 | tf_op jit(solution)/shard_map/scatter | solution.py:119
  782.4 46.1 %collective-permute-done = f32[1024,512]{0,1:T(8,128)} collective-permute-done((f32[1024,512]{0,1:T(8,128)S(1)}, f32[1024,512]{0,1:T(8,128)}, u32[]{:S(2)}, u32[]{:S(2)}) %collective-permute-start) | collective-permute-done | bytes 2097184 | tf_op jit(solution)/shard_map/ppermute | solution.py:12
  828.5 7.3 maximum_select_fusion.1
  838.4 180.4 %collective-permute-done.1 = f32[2048,512]{0,1:T(8,128)} collective-permute-done((f32[2048,512]{0,1:T(8,128)}, f32[2048,512]{0,1:T(8,128)}, u32[]{:S(2)}, u32[]{:S(2)}) %collective-permute-start.1) | collective-permute-done | bytes 4194336 | tf_op jit(solution)/shard_map/ppermute | solution.py:12
  1018.7 6.9 maximum_select_fusion
  1031.7 22.7 %all-gather.5.cloned.1.call-done = f32[512,512]{1,0:T(8,128)} async-done(((f32[64,512]{1,0:T(8,128)}), f32[512,512]{1,0:T(8,128)}) %all-gather.5.cloned.1.call-update) | async-done | bytes 1048592 | tf_op jit(solution)/shard_map/all_gather | solution.py:127
  1054.3 32.0 %convolution_subtract_fusion = f32[4096,512]{1,0:T(8,128)} fusion(f32[4096,512]{1,0:T(8,128)} %param.19, f32[4096,512]{0,1:T(8,128)} %copy-done, f32[512,512]{1,0:T(8,128)} %all-gather.5.cloned.1.call-done), kind=kOutput, calls=%fused_computation.32 | convolution fusion | flops 12886999040 | bytes 26214400 | tf_op jit(solution)/shard_map/dot_general | solution.py:128
  (311 shorter events, 204.5 us)
Async XLA Ops:
  7.2 5.5 copy-start.6
  80.8 38.0 %copy-start.3 = (f32[16,64,512]{2,1,0:T(8,128)}, f32[16,64,512]{2,1,0:T(8,128)S(1)}, u32[]{:S(2)}) copy-start(f32[16,64,512]{2,1,0:T(8,128)S(1)} %get-tuple-element.17) | copy-start | bytes 6291460
  118.7 5.0 copy-start.1
  176.4 17.1 %copy-start.2 = (f32[16,512,64]{1,2,0:T(8,128)S(1)}, f32[16,512,64]{1,2,0:T(8,128)}, u32[]{:S(2)}) copy-start(f32[16,512,64]{1,2,0:T(8,128)} %fusion.73) | copy-start | bytes 6291460
  176.4 17.1 %copy-start.4 = (f32[16,64,512]{2,1,0:T(8,128)S(1)}, f32[16,64,512]{2,1,0:T(8,128)}, u32[]{:S(2)}) copy-start(f32[16,64,512]{2,1,0:T(8,128)} %get-tuple-element.33) | copy-start | bytes 6291460
  340.1 7.5 copy-start.9
  340.1 193.9 %all-to-all-start.1 = ((bf16[16,2,32,4096]{3,0,1,2:T(8,128)(2,1)}), bf16[16,2,32,4096]{3,0,1,2:T(8,128)(2,1)}, u32[]{:S(2)}, u32[]{:S(2)}) async-start(bf16[16,2,32,4096]{3,0,1,2:T(8,128)(2,1)} %copy.65), calls=%async_computation.1 | async-start | bytes 16777216 | tf_op jit(solution)/shard_map/all_to_all | solution.py:70
  347.5 265.6 %all-gather.3.cloned.1.call-start = ((), (), s32[]{:S(2)}) async-start(), calls=%async_computation.3 | async-start | bytes 1081344 | tf_op jit(solution)/shard_map/all_gather | solution.py:64
  376.2 31.8 %copy-start.10 = (s32[1792]{0:T(1024)S(1)}, s32[1792]{0:T(1024)}, u32[]{:S(2)}) copy-start(s32[1792]{0:T(1024)} %param.17) | copy-start | bytes 21508
  376.2 49.5 %copy-start.11 = (s32[1792]{0:T(1024)S(1)}, s32[1792]{0:T(1024)}, u32[]{:S(2)}) copy-start(s32[1792]{0:T(1024)} %param.16) | copy-start | bytes 21508
  534.0 71.6 %all-to-all-start = ((s32[32,1,56]{2,1,0:T(1,128)}), s32[32,1,56]{2,1,0:T(1,128)S(1)}, u32[]{:S(2)}, u32[]{:S(2)}) async-start(s32[32,1,56]{2,1,0:T(1,128)} %all_to_all.12), calls=%async_computation | async-start | bytes 32768 | tf_op jit(solution)/shard_map/all_to_all | solution.py:108
  605.6 151.7 %all-to-all-start.2 = ((f32[32,56,512]{2,1,0:T(8,128)}), f32[32,56,512]{2,1,0:T(8,128)}, u32[]{:S(2)}, u32[]{:S(2)}) async-start(f32[32,56,512]{2,1,0:T(8,128)} %bitcast.164), calls=%async_computation.2 | async-start | bytes 7340032 | tf_op jit(solution)/shard_map/all_to_all | solution.py:101
  611.6 442.7 %all-gather.5.cloned.1.call-start = ((), (), s32[]{:S(2)}) async-start(), calls=%async_computation.4 | async-start | bytes 1179648 | tf_op jit(solution)/shard_map/all_gather | solution.py:127
  717.1 40.2 %copy-start.8 = (f32[512,512]{1,0:T(8,128)}, f32[512,512]{1,0:T(8,128)S(1)}, u32[]{:S(2)}) copy-start(f32[512,512]{1,0:T(8,128)S(1)} %get-tuple-element.333) | copy-start | bytes 3145732
  775.4 4.5 copy-start.5
  779.9 0.8 copy-start.7
  780.7 47.8 %collective-permute-start = (f32[1024,512]{0,1:T(8,128)S(1)}, f32[1024,512]{0,1:T(8,128)}, u32[]{:S(2)}, u32[]{:S(2)}) collective-permute-start(f32[1024,512]{0,1:T(8,128)S(1)} %pad_maximum_fusion), channel_id=1, source_target_pairs={{0,1},{1,0},{2,3},{3,2},{4,5},{5,4},{6,7},{7,6},{8,9},{9,8},{10,11... | collective-permute-start | bytes 6291464 | tf_op jit(solution)/shard_map/ppermute | solution.py:12
  835.8 182.9 %collective-permute-start.1 = (f32[2048,512]{0,1:T(8,128)}, f32[2048,512]{0,1:T(8,128)}, u32[]{:S(2)}, u32[]{:S(2)}) collective-permute-start(f32[2048,512]{0,1:T(8,128)} %maximum_select_fusion.1), channel_id=1, source_target_pairs={{0,2},{1,3},{2,0},{3,1},{4,6},{5,7},{6,4},{7,5},{8,10},{9,11},{10,... | collective-permute-start | bytes 12582920 | tf_op jit(solution)/shard_map/ppermute | solution.py:12
  1025.7 3.2 copy-start
Sparse Core Ops, SparseCore 0:
  407.5 96.1 all-gather.2
  1030.0 24.3 all-gather.4
